TPU v7x, 512 devices: a whole 4x4x16 slice. The times are simulated.
512 devices in a mesh: row: 16 (over z), col: 16 (over y, x), rep: 2 (over core).
Axes of the slice: x: 4, y: 4, z: 16, core: 2. Of those that a mesh axis runs over, the one named last changes fastest.
Arguments:
- tokens: bfloat16 [512, 4096], P(('col', 'rep'), 'row'), may hold values from -6 to 6
- grad_out: bfloat16 [512, 4096], P(('col', 'rep'), 'row'), may hold values from -2.5 to 2.5
- gate_weight: bfloat16 [4096, 14336], P('row', 'col'), may hold values from -0.09375 to 0.09375
- up_weight: bfloat16 [4096, 14336], P('row', 'col'), may hold values from -0.09375 to 0.09375
- down_weight: bfloat16 [14336, 4096], P('col', 'row'), may hold values from -0.046875 to 0.046875
- gate_keep: int32 [32, 112], P('row', 'col'), may hold values from 0 to 1, as said below
- up_keep: int32 [32, 112], P('row', 'col'), may hold values from 0 to 1, as said below
- down_keep: int32 [112, 32], P('col', 'row'), may hold values from 0 to 1, as said below
Outputs:
- mixed: bfloat16 [512, 4096], P(('col', 'rep'), 'row')
- input_grad: bfloat16 [512, 4096], P(('col', 'rep'), 'row')
- gate_weight_grad: bfloat16 [4096, 14336], P('row', 'col')
- up_weight_grad: bfloat16 [4096, 14336], P('row', 'col')
- down_weight_grad: bfloat16 [14336, 4096], P('col', 'row')
Inputs may be any that keep to these rules, and one draw needn't show every extreme that they name: `gate_keep`: 1 keeps the 128 x 128 block of the gate projection, 0 prunes it; the kept share differs from one device's region to the next. `up_keep`: 1 keeps the 128 x 128 block of the up projection, 0 prunes it; the kept share differs from one device's region to the next. `down_keep`: 1 keeps the 128 x 128 block of the down projection, 0 prunes it; the kept share differs from one device's region to the next.
All inputs are finite; a program needn't handle non-finite values.
Results may differ from a plain program's by a relative error of at most 0.025.
Values may be sent and summed in bfloat16 or wider, within the bound.
No kernel may reach another device: no remote copies, remote signals or barrier semaphores. Data moves between devices by JAX's collectives and lax.ppermute only.
A program may use at most 64 MiB of HBM per device.

v0:
```python
import jax
import jax.numpy as jnp
from jax import lax
from jax.sharding import PartitionSpec as P

PLAIN = (((1,), (0,)), ((), ()))
FLIPPED = (((1,), (1,)), ((), ()))
OVER_ROWS = (((0,), (0,)), ((), ()))


def masked(weight, keep):
    rows, cols = keep.shape
    tiled = weight.reshape(rows, weight.shape[0] // rows, cols, weight.shape[1] // cols)
    return (tiled * keep[:, None, :, None].astype(weight.dtype)).reshape(weight.shape)


def product(left, weight, flipped):
    return lax.dot_general(
        left, weight, FLIPPED if flipped else PLAIN, preferred_element_type=jnp.float32
    )


def swiglu_grads(back, gate_value, gate_sig, up_value):
    gate_grad = (back * up_value * gate_sig * (1.0 + gate_value * (1.0 - gate_sig))).astype(
        jnp.bfloat16
    )
    up_grad = (back * gate_value * gate_sig).astype(jnp.bfloat16)
    return (gate_grad, up_grad)


def per_device(
    tokens, grad_out, gate_weight, up_weight, down_weight, gate_keep, up_keep, down_keep
):
    model_block = tokens.shape[1]
    gate_used = masked(gate_weight, gate_keep)
    up_used = masked(up_weight, up_keep)
    down_used = masked(down_weight, down_keep)
    token_panel, grad_panel = (
        lax.all_gather(tokens, "col", axis=0, tiled=True),
        lax.all_gather(grad_out, "col", axis=0, tiled=True),
    )
    gate_part = product(token_panel, gate_used, False)
    up_part = product(token_panel, up_used, False)
    gate_sum, up_sum = (
        lax.psum(gate_part.astype(jnp.bfloat16), "row").astype(jnp.float32),
        lax.psum(up_part.astype(jnp.bfloat16), "row").astype(jnp.float32),
    )
    gate_sig = jax.nn.sigmoid(gate_sum)
    hidden = (gate_sum * gate_sig * up_sum).astype(jnp.bfloat16)
    back_part = product(grad_panel, down_used, True)
    back_sum = lax.psum(back_part.astype(jnp.bfloat16), "row").astype(jnp.float32)
    gate_grad, up_grad = swiglu_grads(back_sum, gate_sum, gate_sig, up_sum)
    gate_term = masked(
        lax.dot_general(token_panel, gate_grad, OVER_ROWS, preferred_element_type=jnp.float32),
        gate_keep,
    )
    up_term = masked(
        lax.dot_general(token_panel, up_grad, OVER_ROWS, preferred_element_type=jnp.float32),
        up_keep,
    )
    down_term = masked(
        lax.dot_general(hidden, grad_panel, OVER_ROWS, preferred_element_type=jnp.float32),
        down_keep,
    )
    gate_total, up_total, down_total = (
        lax.psum(gate_term.astype(jnp.bfloat16), "rep").astype(jnp.float32),
        lax.psum(up_term.astype(jnp.bfloat16), "rep").astype(jnp.float32),
        lax.psum(down_term.astype(jnp.bfloat16), "rep").astype(jnp.float32),
    )
    forward = product(hidden, down_used, False)
    backward = product(gate_grad, gate_used, True) + product(up_grad, up_used, True)
    combined = lax.psum_scatter(
        jnp.concatenate([forward, backward], axis=1).astype(jnp.bfloat16),
        "col",
        scatter_dimension=0,
        tiled=True,
    ).astype(jnp.float32)
    mixed = combined[:, :model_block].astype(jnp.bfloat16)
    input_grad = combined[:, model_block:].astype(jnp.bfloat16)
    return (
        mixed,
        input_grad,
        gate_total.astype(jnp.bfloat16),
        up_total.astype(jnp.bfloat16),
        down_total.astype(jnp.bfloat16),
    )


def solution(mesh):
    return jax.shard_map(
        per_device,
        mesh=mesh,
        in_specs=(
            P(("col", "rep"), "row"),
            P(("col", "rep"), "row"),
            P("row", "col"),
            P("row", "col"),
            P("col", "row"),
            P("row", "col"),
            P("row", "col"),
            P("col", "row"),
        ),
        out_specs=(
            P(("col", "rep"), "row"),
            P(("col", "rep"), "row"),
            P("row", "col"),
            P("row", "col"),
            P("col", "row"),
        ),
        check_vma=False,
    )
```

profile of v0, /device:TPU:1, one launch (start us, length us, event | category | flops | bytes accessed | tf_op | source)
XLA Modules:
  0.0 352.1 jit_solution(348218787414217468)
XLA Ops:
  7.2 0.0 all-reduce.5.cloned.1.call-start
  7.2 19.6 %all_gather.6 = bf16[256,256]{1,0:T(8,128)(2,1)S(1)} all-gather(bf16[16,256]{1,0:T(8,128)(2,1)} %param.8), channel_id=1, replica_groups=mesh['row'=16,'col'=16,'rep'=2] {'col'}, dimensions={0}, use_global_device_ids=true | all-gather | bytes 139264 | tf_op jit(solution)/shard_map/all_gather | solution.py:39
  26.9 0.0 copy-start.4
  26.9 1.3 copy.36
  28.2 0.1 copy.35
  28.3 17.7 %all_gather.7 = bf16[256,256]{1,0:T(8,128)(2,1)S(1)} all-gather(bf16[16,256]{1,0:T(8,128)(2,1)S(1)} %copy-done.8), channel_id=1, replica_groups=mesh['row'=16,'col'=16,'rep'=2] {'col'}, dimensions={0}, use_global_device_ids=true | all-gather | bytes 139264 | tf_op jit(solution)/shard_map/all_gather | solution.py:40
  46.0 0.1 copy.37
  46.1 0.2 copy.34
  46.4 0.5 copy-done.11
  46.8 0.1 copy.33
  46.9 0.3 mul.94
  47.2 1.1 fusion.6
  48.3 0.3 mul.90
  48.7 1.1 fusion.5
  49.7 0.3 mul.98
  50.0 0.7 copy-done.7
  50.8 1.1 fusion.7
  51.9 0.0 all-reduce.5.cloned.1.call-update
  51.9 0.0 reduce-scatter.4.cloned.1.call-start
  51.9 0.1 copy.38
  52.0 0.1 copy.39
  52.1 0.1 copy.40
  52.2 144.1 %all-reduce.5.cloned.1.call-done = (bf16[256,896]{0,1:T(8,128)(2,1)}, bf16[256,896]{0,1:T(8,128)(2,1)}, bf16[256,896]{0,1:T(8,128)(2,1)}) async-done(((bf16[256,896]{0,1:T(8,128)(2,1)}, bf16[256,896]{0,1:T(8,128)(2,1)}, bf16[256,896]{0,1:T(8,128)(2,1)}), (bf16[256,896]{0,1:T(8,128)(2,1)}, bf16[256,896]{0,1:T(8,128)(2,1)}, bf16[256,896]{0,1:T(8,128)(2,1)})) %all-reduce.5.cloned.1.call-update) | async-done | bytes 1376272 | tf_op jit(solution)/shard_map/psum | solution.py:46
  196.3 2.0 convolution_convert_fusion.3
  198.3 0.0 copy-done
  198.3 0.0 copy-done.1
  198.3 0.0 copy-done.2
  198.3 0.4 fusion.12
  198.8 0.4 fusion.19
  199.1 0.6 fusion.8
  199.8 0.8 copy.45
  200.6 0.0 reduce-scatter.4.cloned.1.call-update
  200.6 0.0 all-reduce.7.cloned.1.call-start
  200.7 0.3 mul.110
  201.0 0.7 copy-done.3
  201.6 1.2 fusion.3
  202.8 0.3 mul.107
  203.1 1.1 fusion.4
  204.2 0.3 mul.113
  204.5 1.2 fusion.2
  205.7 0.0 all-reduce.7.cloned.1.call-update
  205.7 88.4 %reduce-scatter.4.cloned.1.call-done = bf16[16,512]{1,0:T(8,128)(2,1)} async-done(((bf16[256,512]{1,0:T(8,128)(2,1)}), bf16[16,512]{1,0:T(8,128)(2,1)}) %reduce-scatter.4.cloned.1.call-update) | async-done | bytes 16400
  294.1 1.3 fusion.24
  295.5 46.3 %all-reduce.7.cloned.1.call-done = (bf16[256,896]{0,1:T(8,128)(2,1)}, bf16[256,896]{0,1:T(8,128)(2,1)}, bf16[896,256]{1,0:T(8,128)(2,1)}) async-done(((bf16[256,896]{0,1:T(8,128)(2,1)}, bf16[256,896]{0,1:T(8,128)(2,1)}, bf16[896,256]{1,0:T(8,128)(2,1)}), (bf16[256,896]{0,1:T(8,128)(2,1)}, bf16[256,896]{0,1:T(8,128)(2,1)}, bf16[896,256]{1,0:T(8,128)(2,1)})) %all-reduce.7.cloned.1.call-update) | async-done | bytes 1376272 | tf_op jit(solution)/shard_map/psum | solution.py:66
  341.8 2.0 copy.43
  343.8 1.0 copy.44
  344.8 0.0 copy-done.5
  344.8 0.8 copy.73
  (20 shorter events, 0.1 us)
Async XLA Ops:
  7.2 189.1 %all-reduce.5.cloned.1.call-start = ((), (), s32[]{:S(2)}) async-start(), calls=%async_computation.2 | async-start | bytes 2752512 | tf_op jit(solution)/shard_map/psum | solution.py:46
  26.8 1.3 copy-start.9
  26.9 1.4 copy-start.8
  26.9 19.3 %copy-start.4 = (bf16[256,896]{1,0:T(8,128)(2,1)S(1)}, bf16[256,896]{1,0:T(8,128)(2,1)}, u32[]{:S(2)}) copy-start(bf16[256,896]{1,0:T(8,128)(2,1)} %param.10) | copy-start | bytes 1376260
  28.3 17.7 %copy-start.10 = (s32[7,2]{0,1:T(2,128)S(1)}, s32[7,2]{0,1:T(2,128)}, u32[]{:S(2)}) copy-start(s32[7,2]{0,1:T(2,128)} %param.15) | copy-start | bytes 172
  46.1 0.7 copy-start.11
  49.7 1.0 copy-start.7
  51.9 242.3 %reduce-scatter.4.cloned.1.call-start = ((), (), s32[]{:S(2)}) async-start(), calls=%async_computation.1 | async-start | bytes 278528
  196.3 2.0 copy-start
  196.3 2.0 copy-start.1
  196.3 2.0 copy-start.2
  200.6 1.0 copy-start.3
  200.6 141.1 %all-reduce.7.cloned.1.call-start = ((), (), s32[]{:S(2)}) async-start(), calls=%async_computation.3 | async-start | bytes 2752512 | tf_op jit(solution)/shard_map/psum | solution.py:66
  341.8 2.0 copy-start.6
  343.8 1.0 copy-start.5
Sparse Core Ops, SparseCore 0:
  52.0 144.2 all-reduce.4
  200.7 93.3 reduce-scatter.3
  297.8 43.9 all-reduce.6
where the time goes:
time: 353 us; the launch traced here: 352 us
  waiting for transfers between devices  279 us (79%)
  blocking collectives  37.4 us (11%)
  between operations  13.9 us (4%)
  local copies, waits for them, and re-layouts  11.7 us (3%)
  matrix products  9.67 us (3%)
    psum x1, waiting for transfers between devices, per_device(): lax.psum(up_part.astype(jnp.bfloat16), 'row').astype(jnp.float32)  144 us
    unnamed x4, waiting for transfers between devices  88.5 us
    psum x1, waiting for transfers between devices, per_device(): lax.psum(gate_term.astype(jnp.bfloat16), 'rep').astype(jnp.float32)  46.3 us
    all_gather x1, blocking collectives, per_device(): lax.all_gather(tokens, 'col', axis=0, tiled=True)  19.6 us
    all_gather x1, blocking collectives, per_device(): lax.all_gather(grad_out, 'col', axis=0, tiled=True)  17.7 us
    unnamed x30, local copies, waits for them, and re-layouts  8.01 us
  transfers between devices with their start and end apart: 3, of which 3 were waited for; matrix products, arithmetic and copies ran while one was open for 2% of the time, Pallas kernels for 0%

commit v1 on v0

--- a/solution.py
+++ b/solution.py
@@ -6,6 +6,13 @@
 PLAIN = (((1,), (0,)), ((), ()))
 FLIPPED = (((1,), (1,)), ((), ()))
 OVER_ROWS = (((0,), (0,)), ((), ()))
+
+
+def all_by_exchange(value, axis, dim):
+    devices = lax.axis_size(axis)
+    blocks = jnp.stack([value for _ in range(devices)])
+    blocks = lax.all_to_all(blocks, axis, split_axis=0, concat_axis=0)
+    return jnp.concatenate(blocks, axis=dim)
 
 
 def masked(weight, keep):
@@ -37,7 +44,7 @@
     down_used = masked(down_weight, down_keep)
     token_panel, grad_panel = (
         lax.all_gather(tokens, "col", axis=0, tiled=True),
-        lax.all_gather(grad_out, "col", axis=0, tiled=True),
+        all_by_exchange(grad_out, "col", 0),
     )
     gate_part = product(token_panel, gate_used, False)
     up_part = product(token_panel, up_used, False)

time: 353 us -> 339 us (0.960)
  blocking collectives: 37.4 us -> 19.1 us
  starting transfers between devices: 0.12 us -> 7.7 us
  waiting for transfers between devices: 279 us -> 274 us
    all_gather x1 -> x0, blocking collectives: 17.7 us -> none  [per_device(): lax.all_gather(grad_out, 'col', axis=0, tiled=True)]
    all_to_all x0 -> x1, starting transfers between devices: none -> 7.57 us  [all_by_exchange(): blocks = lax.all_to_all(blocks, axis, split_axis=0, concat_axis=0)]
    psum x1, waiting for transfers between devices: 144 us -> 139 us  [per_device(): lax.psum(up_part.astype(jnp.bfloat16), 'row').astype(jnp.float32)]
    unnamed x30 -> x33, local copies, waits for them, and re-layouts: 8.01 us -> 9.75 us
  transfers between devices with their start and end apart: 3 -> 4, of which waited for: 3 -> 3; matrix products, arithmetic and copies ran while one was open for 2% -> 3% of each run, Pallas kernels for 0% -> 0%
where the time goes in v1:
time: 339 us; the launch traced here: 338 us
  waiting for transfers between devices  274 us (81%)
  blocking collectives  19.1 us (6%)
  local copies, waits for them, and re-layouts  15.2 us (4%)
  between operations  13.9 us (4%)
  starting transfers between devices  7.7 us (2%)
  matrix products  7.15 us (2%)
    psum x1, waiting for transfers between devices, per_device(): lax.psum(up_part.astype(jnp.bfloat16), 'row').astype(jnp.float32)  139 us
    unnamed x4, waiting for transfers between devices  88.1 us
    psum x1, waiting for transfers between devices, per_device(): lax.psum(gate_term.astype(jnp.bfloat16), 'rep').astype(jnp.float32)  46.3 us
    all_gather x1, blocking collectives, per_device(): lax.all_gather(tokens, 'col', axis=0, tiled=True)  19.1 us
    unnamed x33, local copies, waits for them, and re-layouts  9.75 us
    all_to_all x1, starting transfers between devices, all_by_exchange(): blocks = lax.all_to_all(blocks, axis, split_axis=0, concat_axis=0)  7.57 us
  transfers between devices with their start and end apart: 4, of which 3 were waited for; matrix products, arithmetic and copies ran while one was open for 3% of the time, Pallas kernels for 0%

profile of v1, /device:TPU:1, one launch (start us, length us, event | category | flops | bytes accessed | tf_op | source)
XLA Modules:
  0.0 338.4 jit_solution(14850863060494846317)
XLA Ops:
  7.2 1.4 stack.2
  8.6 7.6 %all-to-all-start = ((bf16[16,16,256]{2,1,0:T(8,128)(2,1)}), bf16[16,16,256]{2,1,0:T(8,128)(2,1)S(1)}, u32[]{:S(2)}, u32[]{:S(2)}) async-start(bf16[16,16,256]{2,1,0:T(8,128)(2,1)} %stack.2), calls=%async_computation | async-start | bytes 262144 | tf_op jit(solution)/shard_map/all_to_all | solution.py:14
  16.2 19.1 %all_gather.3 = bf16[256,256]{1,0:T(8,128)(2,1)S(1)} all-gather(bf16[16,256]{1,0:T(8,128)(2,1)} %param.8), channel_id=1, replica_groups=mesh['row'=16,'col'=16,'rep'=2] {'col'}, dimensions={0}, use_global_device_ids=true | all-gather | bytes 139264 | tf_op jit(solution)/shard_map/all_gather | solution.py:46
  35.4 0.2 copy.39
  35.6 0.4 copy-done.10
  36.0 0.1 copy.38
  36.2 0.2 copy-done.1
  36.4 0.2 copy.37
  36.6 0.5 copy-done.11
  37.1 0.1 copy.36
  37.2 0.3 mul.91
  37.5 1.1 fusion.6
  38.6 0.3 mul.87
  38.9 1.1 fusion.5
  40.0 0.1 copy.40
  40.1 0.3 mul.95
  40.5 0.6 copy-done.4
  41.0 1.1 fusion.7
  42.2 0.0 reduce-scatter.4.cloned.1.call-start
  42.2 0.1 copy.41
  42.3 0.1 copy.42
  42.4 0.1 copy.44
  42.5 0.1 copy.43
  42.6 139.1 %all-reduce.5.cloned.1.call-done = (bf16[256,896]{0,1:T(8,128)(2,1)}, bf16[256,896]{0,1:T(8,128)(2,1)}, bf16[256,896]{0,1:T(8,128)(2,1)}) async-done(((bf16[256,896]{0,1:T(8,128)(2,1)}, bf16[256,896]{0,1:T(8,128)(2,1)}, bf16[256,896]{0,1:T(8,128)(2,1)}), (bf16[256,896]{0,1:T(8,128)(2,1)}, bf16[256,896]{0,1:T(8,128)(2,1)}, bf16[256,896]{0,1:T(8,128)(2,1)})) %all-reduce.5.cloned.1.call-update) | async-done | bytes 1376272 | tf_op jit(solution)/shard_map/psum | solution.py:53
  181.7 1.8 fusion.9
  183.5 0.4 fusion.19
  183.8 0.6 copy-done.6
  184.5 0.1 copy-done.8
  184.6 0.6 fusion.8
  185.2 0.4 copy-done.5
  185.6 0.4 convolution_convert_fusion.3
  186.0 0.9 copy.51
  186.9 0.3 fusion.2
  187.3 0.5 copy.45
  187.8 0.8 copy.73
  188.6 0.3 mul.104
  188.9 1.1 fusion.4
  190.0 0.3 mul.107
  190.3 0.7 copy-done.7
  191.0 0.1 copy-done.9
  191.1 1.2 fusion.3
  192.3 88.1 %reduce-scatter.4.cloned.1.call-done = bf16[16,512]{1,0:T(8,128)(2,1)} async-done(((bf16[256,512]{1,0:T(8,128)(2,1)}), bf16[16,512]{1,0:T(8,128)(2,1)}) %reduce-scatter.4.cloned.1.call-update) | async-done | bytes 16400
  280.4 1.3 fusion.22
  281.7 46.3 %all-reduce.7.cloned.1.call-done = (bf16[256,896]{0,1:T(8,128)(2,1)}, bf16[256,896]{0,1:T(8,128)(2,1)}, bf16[896,256]{1,0:T(8,128)(2,1)}) async-done(((bf16[256,896]{0,1:T(8,128)(2,1)}, bf16[256,896]{0,1:T(8,128)(2,1)}, bf16[896,256]{1,0:T(8,128)(2,1)}), (bf16[256,896]{0,1:T(8,128)(2,1)}, bf16[256,896]{0,1:T(8,128)(2,1)}, bf16[896,256]{1,0:T(8,128)(2,1)})) %all-reduce.7.cloned.1.call-update) | async-done | bytes 1376272 | tf_op jit(solution)/shard_map/psum | solution.py:73
  328.0 2.0 copy.48
  330.1 1.0 copy.49
  331.1 0.0 copy-done.2
  331.1 0.8 copy.80
  (26 shorter events, 0.2 us)
Async XLA Ops:
  7.2 28.2 %copy-start = (bf16[256,896]{1,0:T(8,128)(2,1)S(1)}, bf16[256,896]{1,0:T(8,128)(2,1)}, u32[]{:S(2)}) copy-start(bf16[256,896]{1,0:T(8,128)(2,1)} %param.11) | copy-start | bytes 1376260
  8.6 31.5 %all-to-all-start = ((bf16[16,16,256]{2,1,0:T(8,128)(2,1)}), bf16[16,16,256]{2,1,0:T(8,128)(2,1)S(1)}, u32[]{:S(2)}, u32[]{:S(2)}) async-start(bf16[16,16,256]{2,1,0:T(8,128)(2,1)} %stack.2), calls=%async_computation | async-start | bytes 262144 | tf_op jit(solution)/shard_map/all_to_all | solution.py:14
  16.2 165.5 %all-reduce.5.cloned.1.call-start = ((), (), s32[]{:S(2)}) async-start(), calls=%async_computation.3 | async-start | bytes 2752512 | tf_op jit(solution)/shard_map/psum | solution.py:53
  35.4 0.7 copy-start.10
  35.4 1.0 copy-start.1
  36.4 0.7 copy-start.11
  38.9 1.1 copy-start.12
  40.0 1.0 copy-start.4
  42.2 238.3 %reduce-scatter.4.cloned.1.call-start = ((), (), s32[]{:S(2)}) async-start(), calls=%async_computation.2 | async-start | bytes 278528
  183.5 1.0 copy-start.6
  183.5 1.1 copy-start.8
  184.6 1.0 copy-start.5
  186.9 141.1 %all-reduce.7.cloned.1.call-start = ((), (), s32[]{:S(2)}) async-start(), calls=%async_computation.4 | async-start | bytes 2752512 | tf_op jit(solution)/shard_map/psum | solution.py:73
  190.0 1.0 copy-start.7
  190.0 1.2 copy-start.9
  328.0 2.0 copy-start.3
  330.1 1.0 copy-start.2
Sparse Core Ops, SparseCore 0:
  42.3 139.3 all-reduce.4
  187.0 93.3 reduce-scatter.3
  284.1 43.9 all-reduce.6
